TPU v7x, 128 devices: a whole 4x4x4 slice. The times are simulated.
128 devices in a mesh: smp: 32 (over x, z, y_lo), col: 2 (over core), slab: 2 (over y_hi).
Axes of the slice: x: 4, y: 4 (y_hi: 2, y_lo: 2; y = y_hi * 2 + y_lo), z: 4, core: 2. Of those that a mesh axis runs over, the one named last changes fastest.
Arguments:
- jacobian: bfloat16 [1024, 32, 16384], P('smp', 'slab', 'col'), may hold values from -0.005722046 to 0.005722046
- local_energy: float32 [1024], P('smp'), may hold values from -6 to 6
Outputs:
- update: float32 [32, 16384], P('slab', ('col', 'smp'))
All inputs are finite; a program needn't handle non-finite values.
Results may differ from a plain program's by a relative error of at most 0.0085.
Values may be sent and summed in bfloat16 or wider, within the bound.
A program may use at most 192 MiB of HBM per device.

v0:
```python
import jax
import jax.numpy as jnp
from jax import lax
from jax.sharding import PartitionSpec as P

SLABS = 32
SLAB_COLS = 16384


def shards(jacobian, local_energy):
    energies = lax.all_gather(local_energy, "smp", axis=0, tiled=True)
    samples = energies.shape[0]
    root_count = jnp.sqrt(jnp.float32(samples))
    eps = (energies - jnp.mean(energies)) / root_count
    columns = lax.all_to_all(jacobian, "smp", split_axis=2, concat_axis=0, tiled=True)
    slab_count = columns.shape[1]
    width = columns.shape[2]
    values = columns.astype(jnp.float32)
    mean_row = jnp.mean(values, axis=0, keepdims=True)
    centered = (
        ((values - mean_row) / root_count).astype(jnp.bfloat16).reshape(samples, slab_count * width)
    )
    partial_gram = jnp.dot(centered, centered.T, preferred_element_type=jnp.float32)
    gram = lax.psum(partial_gram, ("smp", "col", "slab"))
    shift = 0.01 * jnp.trace(gram) / samples
    factor = jnp.linalg.cholesky(gram + shift * jnp.eye(samples, dtype=jnp.float32))
    middle = lax.linalg.triangular_solve(factor, eps[:, None], left_side=True, lower=True)
    coeffs = lax.linalg.triangular_solve(
        factor, middle, left_side=True, lower=True, transpose_a=True
    )[:, 0]
    delta = jnp.dot(coeffs, centered.astype(jnp.float32), precision=lax.Precision.HIGHEST)
    squared = lax.psum(jnp.sum(delta * delta), ("smp", "col", "slab"))
    limit = 0.3 * jnp.sqrt(jnp.float32(SLABS * SLAB_COLS))
    scaled = -jnp.minimum(1.0, limit / jnp.sqrt(squared)) * delta
    return scaled.reshape(slab_count, width)


def solution(mesh):
    in_specs = (P("smp", "slab", "col"), P("smp"))
    out_specs = P("slab", ("col", "smp"))
    return jax.shard_map(shards, mesh=mesh, in_specs=in_specs, out_specs=out_specs, check_vma=False)
```

profile of v0, /device:TPU:1, one launch (start us, length us, event | category | flops | bytes accessed | tf_op | source)
XLA Modules:
  0.0 897.0 jit_solution(18186082243385075913)
XLA Ops:
  6.5 45.6 %copy.65 = bf16[32,16,8192]{0,1,2:T(8,128)(2,1)} copy(bf16[32,16,8192]{2,1,0:T(8,128)(2,1)} %param.2) | data formatting | bytes 16777216 | tf_op args[0]
  52.1 39.8 %reshape.341 = bf16[32,2,65536]{2,1,0:T(2,128)(2,1)} reshape(bf16[8192,16,32]{2,1,0:T(8,128)(2,1)} %bitcast.340) | data formatting | bytes 16777216
  91.9 105.1 %all_to_all.4 = bf16[32,2,65536]{2,1,0:T(2,128)(2,1)} all-to-all(bf16[32,2,65536]{2,1,0:T(2,128)(2,1)} %reshape.341), channel_id=1, replica_groups=mesh['smp'=32,'col'=2,'slab'=2] {'smp'}, dimensions={0} | all-to-all | bytes 16777216 | tf_op jit(solution)/shard_map/all_to_all | solution.py:15
  197.0 30.6 %reshape.342 = bf16[8192,16,32]{2,1,0:T(8,128)(2,1)} reshape(bf16[32,2,65536]{2,1,0:T(2,128)(2,1)} %all_to_all.4) | data formatting | bytes 16777216
  227.6 44.0 %copy.66 = f32[32,16,32,256]{3,1,0,2:T(8,128)} copy(bf16[32,16,32,256]{0,1,3,2:T(8,128)(2,1)} %bitcast.339) | data formatting | bytes 25165824 | tf_op jit(solution)/shard_map/convert_element_type | solution.py:18
  271.6 6.9 bitcast_reduce_fusion
  278.5 7.2 fusion.1
  285.7 3.2 copy-done
  288.9 16.6 %fusion.5 = f32[1024,1024]{0,1:T(8,128)} fusion(bf16[1024,16,256]{2,1,0:T(8,128)(2,1)S(1)} %bitcast.342), kind=kOutput, calls=%fused_computation.15 | convolution fusion | flops 8589934592 | bytes 12582912 | tf_op jit(solution)/shard_map/dot_general | solution.py:23
  307.8 65.8 %all-reduce.1 = f32[1024]{0:T(1024)S(1)} all-reduce(f32[1024]{0:T(1024)S(1)} %dynamic-update-slice.47), channel_id=1, replica_groups=mesh['smp'=32,'col'=2,'slab'=2] {'smp'}, use_global_device_ids=true, to_apply=%add.1 | all-reduce | flops 1024 | bytes 8192
  375.0 12.3 %copy.96 = bf16[128,8,16,256]{3,1,2,0:T(8,128)(2,1)} copy(bf16[128,8,16,256]{3,2,1,0:T(8,128)(2,1)} %bitcast.343) | data formatting | bytes 16777216
  387.3 73.0 %all-reduce.4.cloned.1.call-done = f32[1024,1024]{0,1:T(8,128)} async-done(((f32[1024,1024]{0,1:T(8,128)}), f32[1024,1024]{0,1:T(8,128)}) %all-reduce.4.cloned.1.call-update) | async-done | bytes 4194320 | tf_op jit(solution)/shard_map/psum | solution.py:24
  460.3 2.9 select_reduce_fusion
  463.8 4.8 select_add_fusion
  468.6 5.5 copy.70
  474.1 4.5 fusion.4
  480.6 11.7 %cholesky.222 = f32[128,128]{1,0:T(8,128)S(1)} custom-call(f32[128,128]{1,0:T(8,128)S(1)} %cholesky.577), custom_call_target="Cholesky" | custom-call | tf_op jit(solution)/shard_map/jit(cholesky)/cholesky | solution.py:26
  492.3 9.8 %custom-call.64 = f32[1,128,128]{1,2,0:T(8,128)S(1)} custom-call(f32[1,128,128]{2,1,0:T(8,128)S(1)} %get-tuple-element.52), custom_call_target="InvertDiagBlocksLowerTriangular" | custom-call | tf_op jit(solution)/shard_map/jit(cholesky)/cholesky | solution.py:26
  505.3 11.7 %cholesky.243 = f32[128,128]{1,0:T(8,128)S(1)} custom-call(f32[128,128]{1,0:T(8,128)S(1)} %cholesky.581), custom_call_target="Cholesky" | custom-call | tf_op jit(solution)/shard_map/jit(cholesky)/cholesky | solution.py:26
  517.8 2.5 cholesky.254
  520.3 9.8 %custom-call.65 = f32[1,128,128]{1,2,0:T(8,128)S(1)} custom-call(f32[1,128,128]{2,1,0:T(8,128)S(1)} %get-tuple-element.50), custom_call_target="InvertDiagBlocksLowerTriangular" | custom-call | tf_op jit(solution)/shard_map/jit(cholesky)/cholesky | solution.py:26
  532.9 2.7 convolution_subtract_fusion.1
  535.6 11.7 %cholesky.466 = f32[128,128]{1,0:T(8,128)S(1)} custom-call(f32[128,128]{1,0:T(8,128)S(1)} %cholesky.586), custom_call_target="Cholesky" | custom-call | tf_op jit(solution)/shard_map/jit(cholesky)/cholesky | solution.py:26
  548.1 9.8 %custom-call.66 = f32[1,128,128]{1,2,0:T(8,128)S(1)} custom-call(f32[1,128,128]{2,1,0:T(8,128)S(1)} %get-tuple-element.48), custom_call_target="InvertDiagBlocksLowerTriangular" | custom-call | tf_op jit(solution)/shard_map/jit(cholesky)/cholesky | solution.py:26
  559.2 3.3 convolution_subtract_fusion.2
  562.5 11.7 %cholesky.485 = f32[128,128]{1,0:T(8,128)S(1)} custom-call(f32[128,128]{1,0:T(8,128)S(1)} %cholesky.591), custom_call_target="Cholesky" | custom-call | tf_op jit(solution)/shard_map/jit(cholesky)/cholesky | solution.py:26
  575.0 9.8 %custom-call.67 = f32[1,128,128]{1,2,0:T(8,128)S(1)} custom-call(f32[1,128,128]{2,1,0:T(8,128)S(1)} %get-tuple-element.46), custom_call_target="InvertDiagBlocksLowerTriangular" | custom-call | tf_op jit(solution)/shard_map/jit(cholesky)/cholesky | solution.py:26
  585.9 3.2 convolution_subtract_fusion.3
  589.1 11.9 %cholesky.504 = f32[128,128]{1,0:T(8,128)S(1)} custom-call(f32[128,128]{1,0:T(8,128)S(1)} %cholesky.596), custom_call_target="Cholesky" | custom-call | tf_op jit(solution)/shard_map/jit(cholesky)/cholesky | solution.py:26
  601.8 9.8 %custom-call.68 = f32[1,128,128]{1,2,0:T(8,128)S(1)} custom-call(f32[1,128,128]{2,1,0:T(8,128)S(1)} %get-tuple-element.44), custom_call_target="InvertDiagBlocksLowerTriangular" | custom-call | tf_op jit(solution)/shard_map/jit(cholesky)/cholesky | solution.py:26
  612.7 3.1 convolution_subtract_fusion.4
  615.8 11.7 %cholesky.524 = f32[128,128]{1,0:T(8,128)S(1)} custom-call(f32[128,128]{1,0:T(8,128)S(1)} %cholesky.601), custom_call_target="Cholesky" | custom-call | tf_op jit(solution)/shard_map/jit(cholesky)/cholesky | solution.py:26
  628.3 9.8 %custom-call.69 = f32[1,128,128]{1,2,0:T(8,128)S(1)} custom-call(f32[1,128,128]{2,1,0:T(8,128)S(1)} %get-tuple-element.42), custom_call_target="InvertDiagBlocksLowerTriangular" | custom-call | tf_op jit(solution)/shard_map/jit(cholesky)/cholesky | solution.py:26
  639.1 3.1 convolution_subtract_fusion.5
  642.2 11.7 %cholesky.544 = f32[128,128]{1,0:T(8,128)S(1)} custom-call(f32[128,128]{1,0:T(8,128)S(1)} %cholesky.606), custom_call_target="Cholesky" | custom-call | tf_op jit(solution)/shard_map/jit(cholesky)/cholesky | solution.py:26
  654.7 9.8 %custom-call.70 = f32[1,128,128]{1,2,0:T(8,128)S(1)} custom-call(f32[1,128,128]{2,1,0:T(8,128)S(1)} %get-tuple-element.40), custom_call_target="InvertDiagBlocksLowerTriangular" | custom-call | tf_op jit(solution)/shard_map/jit(cholesky)/cholesky | solution.py:26
  667.5 11.7 %cholesky.562 = f32[128,128]{1,0:T(8,128)S(1)} custom-call(f32[128,128]{1,0:T(8,128)S(1)} %convolution_subtract_fusion.6), custom_call_target="Cholesky" | custom-call | tf_op jit(solution)/shard_map/jit(cholesky)/cholesky | solution.py:26
  689.4 4.9 select_select_fusion
  694.3 24.5 %while.1 = (s32[]{:T(128)}, f32[1024,1024]{0,1:T(8,128)}, s32[8,2]{0,1:T(2,128)S(1)}, f32[8,128,128]{2,1,0:T(8,128)S(1)}, s32[]{:T(128)}) while((s32[]{:T(128)}, f32[1024,1024]{0,1:T(8,128)}, s32[8,2]{0,1:T(2,128)S(1)}, f32[8,128,128]{2,1,0:T(8,128)S(1)}, s32[]{:T(128)}) %tuple.52), condition=%wide.while_cond, body=%wide.while_body.sunk | while | flops 2 | bytes 393321 | solution.py:28
  694.9 2.3 dynamic-slice.8
  698.0 2.3 dynamic-slice.8
  701.0 2.3 dynamic-slice.8
  704.1 2.3 dynamic-slice.8
  707.2 2.3 dynamic-slice.8
  710.3 2.3 dynamic-slice.8
  718.7 78.8 %custom-call.71 = f32[8,128,128]{1,2,0:T(8,128)S(1)} custom-call(f32[8,128,128]{2,1,0:T(8,128)S(1)} %get-tuple-element.12), custom_call_target="InvertDiagBlocksLowerTriangular" | custom-call | tf_op jit(solution)/shard_map/triangular_solve | solution.py:28
  818.5 5.7 fusion.125
  824.8 63.9 %psum.15 = f32[]{:T(128)} all-reduce(f32[]{:T(128)} %multiply_reduce_fusion), channel_id=1, replica_groups=mesh['smp'=32,'col'=2,'slab'=2] {'smp','col','slab'}, use_global_device_ids=true, to_apply=%region_21.22 | all-reduce | flops 1 | bytes 8 | tf_op jit(solution)/shard_map/psum | solution.py:32
  (155 shorter events, 60.3 us)
Async XLA Ops:
  6.5 453.8 %all-reduce.4.cloned.1.call-start = ((), (), s32[]{:S(2)}) async-start(), calls=%async_computation.1 | async-start | bytes 8388608 | tf_op jit(solution)/shard_map/psum | solution.py:24
  285.7 3.2 copy-start
  305.5 0.7 copy-start.3
  305.5 2.0 copy-start.2
  478.6 2.0 copy-start.1
Sparse Core Ops, SparseCore 0:
  305.7 154.5 all-reduce.3
where the time goes:
time: 904 us; the launch traced here: 897 us
  other arithmetic  279 us (31%)
  blocking collectives  235 us (26%)
  local copies, waits for them, and re-layouts  219 us (24%)
  waiting for transfers between devices  73 us (8%)
  matrix products  70 us (8%)
  between operations  21.6 us (2%)
    another operation x30, other arithmetic, shards(): jnp.linalg.cholesky(gram + shift * jnp.eye(samples, dtype=jnp.float32))  167 us
    unnamed x33, local copies, waits for them, and re-layouts  135 us
    all_to_all x1, blocking collectives, shards(): lax.all_to_all(jacobian, 'smp', split_axis=2, concat_axis=0, tiled=True)  105 us
    another operation x3, other arithmetic, shards(): lax.linalg.triangular_solve(factor, middle, left_side=True, lower=True, t...  83.6 us
    psum x1, waiting for transfers between devices, shards(): gram = lax.psum(partial_gram, ('smp', 'col', 'slab'))  73 us
    unnamed x1, blocking collectives  65.8 us
    psum x1, blocking collectives, shards(): squared = lax.psum(jnp.sum(delta * delta), ('smp', 'col', 'slab'))  63.9 us
    convert_element_type x1, local copies, waits for them, and re-layouts, shards(): values = columns.astype(jnp.float32)  44 us
  transfers between devices with their start and end apart: 1, of which 1 were waited for; matrix products, arithmetic and copies ran while one was open for 2% of the time, Pallas kernels for 0%

commit v1 on v0

--- a/solution.py
+++ b/solution.py
@@ -12,7 +12,10 @@
     samples = energies.shape[0]
     root_count = jnp.sqrt(jnp.float32(samples))
     eps = (energies - jnp.mean(energies)) / root_count
-    columns = lax.all_to_all(jacobian, "smp", split_axis=2, concat_axis=0, tiled=True)
+    n_dev = lax.axis_size("smp")
+    blocks = jnp.stack(jnp.split(jacobian, n_dev, axis=2), axis=0)
+    blocks = lax.all_to_all(blocks, "smp", split_axis=0, concat_axis=0)
+    columns = jnp.concatenate(blocks, axis=0)
     slab_count = columns.shape[1]
     width = columns.shape[2]
     values = columns.astype(jnp.float32)

time: 904 us -> 782 us (0.87)
  local copies, waits for them, and re-layouts: 219 us -> 89.4 us
    unnamed x33 -> x61, local copies, waits for them, and re-layouts: 135 us -> 48.8 us
    convert_element_type x1 -> x0, local copies, waits for them, and re-layouts: 44 us -> none  [shards(): values = columns.astype(jnp.float32)]
    another operation x40 -> x41, local copies, waits for them, and re-layouts: 24.2 us -> 25.2 us
where the time goes in v1:
time: 782 us; the launch traced here: 770 us
  other arithmetic  275 us (35%)
  blocking collectives  234 us (30%)
  local copies, waits for them, and re-layouts  89.4 us (11%)
  matrix products  76.8 us (10%)
  waiting for transfers between devices  73.2 us (9%)
  between operations  21.6 us (3%)
    another operation x30, other arithmetic, shards(): jnp.linalg.cholesky(gram + shift * jnp.eye(samples, dtype=jnp.float32))  167 us
    all_to_all x1, blocking collectives, shards(): blocks = lax.all_to_all(blocks, 'smp', split_axis=0, concat_axis=0)  104 us
    another operation x3, other arithmetic, shards(): lax.linalg.triangular_solve(factor, middle, left_side=True, lower=True, t...  83.6 us
    psum x1, waiting for transfers between devices, shards(): gram = lax.psum(partial_gram, ('smp', 'col', 'slab'))  73.1 us
    unnamed x1, blocking collectives  66 us
    psum x1, blocking collectives, shards(): squared = lax.psum(jnp.sum(delta * delta), ('smp', 'col', 'slab'))  63.9 us
    unnamed x61, local copies, waits for them, and re-layouts  48.8 us
    another operation x14, matrix products, shards(): jnp.linalg.cholesky(gram + shift * jnp.eye(samples, dtype=jnp.float32))  27.1 us
  transfers between devices with their start and end apart: 1, of which 1 were waited for; matrix products, arithmetic and copies ran while one was open for 2% of the time, Pallas kernels for 0%

profile of v1, /device:TPU:1, one launch (start us, length us, event | category | flops | bytes accessed | tf_op | source)
XLA Modules:
  0.0 769.9 jit_solution(2119023692501416147)
XLA Ops:
  37.7 104.2 %all_to_all.5 = bf16[32,32,16,256]{3,2,1,0:T(8,128)(2,1)S(1)} all-to-all(bf16[32,32,16,256]{3,2,1,0:T(8,128)(2,1)S(1)} %bitcast_dynamic-update-slice_fusion.1), channel_id=1, replica_groups=mesh['smp'=32,'col'=2,'slab'=2] {'smp'}, dimensions={0} | all-to-all | bytes 16777216 | tf_op jit(solution)/shard_map/all_to_all | solution.py:17
  141.9 3.2 copy-done
  146.3 8.9 %fusion.1 = bf16[32,32,16,256]{3,2,1,0:T(8,128)(2,1)} fusion(bf16[32,32,16,256]{3,2,1,0:T(8,128)(2,1)} %copy-done, f32[16,256]{1,0:T(8,128)S(1)} %broadcast_multiply_fusion.1), kind=kLoop, calls=%fused_computation.5 | loop fusion | flops 16777216 | bytes 16793600 | tf_op jit(solution)/shard_map/convert_element_type | solution.py:24
  155.2 23.4 %fusion.5 = f32[1024,1024]{0,1:T(8,128)} fusion(bf16[1024,16,256]{2,1,0:T(8,128)(2,1)} %bitcast.393), kind=kOutput, calls=%fused_computation.15 | convolution fusion | flops 8589934592 | bytes 12582912 | tf_op jit(solution)/shard_map/dot_general | solution.py:26
  180.4 66.0 %all-reduce.1 = f32[1024]{0:T(1024)S(1)} all-reduce(f32[1024]{0:T(1024)S(1)} %dynamic-update-slice.47), channel_id=1, replica_groups=mesh['smp'=32,'col'=2,'slab'=2] {'smp'}, use_global_device_ids=true, to_apply=%add.1 | all-reduce | flops 1024 | bytes 8192
  247.7 12.3 %copy.32 = bf16[128,8,16,256]{3,1,2,0:T(8,128)(2,1)} copy(bf16[128,8,16,256]{3,2,1,0:T(8,128)(2,1)} %bitcast.394) | data formatting | bytes 16777216
  260.0 73.1 %all-reduce.4.cloned.1.call-done = f32[1024,1024]{0,1:T(8,128)} async-done(((f32[1024,1024]{0,1:T(8,128)}), f32[1024,1024]{0,1:T(8,128)}) %all-reduce.4.cloned.1.call-update) | async-done | bytes 4194320 | tf_op jit(solution)/shard_map/psum | solution.py:27
  333.1 2.9 select_reduce_fusion
  336.6 4.8 select_add_fusion
  341.4 5.5 copy.6
  347.0 4.5 fusion.4
  351.4 2.0 copy-done.1
  353.4 11.7 %cholesky.222 = f32[128,128]{1,0:T(8,128)S(1)} custom-call(f32[128,128]{1,0:T(8,128)S(1)} %cholesky.577), custom_call_target="Cholesky" | custom-call | tf_op jit(solution)/shard_map/jit(cholesky)/cholesky | solution.py:29
  365.3 9.8 %custom-call.64 = f32[1,128,128]{1,2,0:T(8,128)S(1)} custom-call(f32[1,128,128]{2,1,0:T(8,128)S(1)} %get-tuple-element.40), custom_call_target="InvertDiagBlocksLowerTriangular" | custom-call | tf_op jit(solution)/shard_map/jit(cholesky)/cholesky | solution.py:29
  376.8 1.6 convolution_subtract_fusion
  378.4 11.7 %cholesky.243 = f32[128,128]{1,0:T(8,128)S(1)} custom-call(f32[128,128]{1,0:T(8,128)S(1)} %cholesky.581), custom_call_target="Cholesky" | custom-call | tf_op jit(solution)/shard_map/jit(cholesky)/cholesky | solution.py:29
  390.6 2.5 cholesky.254
  393.1 9.8 %custom-call.65 = f32[1,128,128]{1,2,0:T(8,128)S(1)} custom-call(f32[1,128,128]{2,1,0:T(8,128)S(1)} %get-tuple-element.38), custom_call_target="InvertDiagBlocksLowerTriangular" | custom-call | tf_op jit(solution)/shard_map/jit(cholesky)/cholesky | solution.py:29
  405.7 2.7 convolution_subtract_fusion.1
  408.5 11.7 %cholesky.466 = f32[128,128]{1,0:T(8,128)S(1)} custom-call(f32[128,128]{1,0:T(8,128)S(1)} %cholesky.586), custom_call_target="Cholesky" | custom-call | tf_op jit(solution)/shard_map/jit(cholesky)/cholesky | solution.py:29
  421.0 9.8 %custom-call.66 = f32[1,128,128]{1,2,0:T(8,128)S(1)} custom-call(f32[1,128,128]{2,1,0:T(8,128)S(1)} %get-tuple-element.36), custom_call_target="InvertDiagBlocksLowerTriangular" | custom-call | tf_op jit(solution)/shard_map/jit(cholesky)/cholesky | solution.py:29
  432.0 3.3 convolution_subtract_fusion.2
  435.3 11.7 %cholesky.485 = f32[128,128]{1,0:T(8,128)S(1)} custom-call(f32[128,128]{1,0:T(8,128)S(1)} %cholesky.591), custom_call_target="Cholesky" | custom-call | tf_op jit(solution)/shard_map/jit(cholesky)/cholesky | solution.py:29
  447.8 9.8 %custom-call.67 = f32[1,128,128]{1,2,0:T(8,128)S(1)} custom-call(f32[1,128,128]{2,1,0:T(8,128)S(1)} %get-tuple-element.34), custom_call_target="InvertDiagBlocksLowerTriangular" | custom-call | tf_op jit(solution)/shard_map/jit(cholesky)/cholesky | solution.py:29
  458.7 3.2 convolution_subtract_fusion.3
  461.9 11.9 %cholesky.504 = f32[128,128]{1,0:T(8,128)S(1)} custom-call(f32[128,128]{1,0:T(8,128)S(1)} %cholesky.596), custom_call_target="Cholesky" | custom-call | tf_op jit(solution)/shard_map/jit(cholesky)/cholesky | solution.py:29
  474.6 9.8 %custom-call.68 = f32[1,128,128]{1,2,0:T(8,128)S(1)} custom-call(f32[1,128,128]{2,1,0:T(8,128)S(1)} %get-tuple-element.32), custom_call_target="InvertDiagBlocksLowerTriangular" | custom-call | tf_op jit(solution)/shard_map/jit(cholesky)/cholesky | solution.py:29
  485.5 3.1 convolution_subtract_fusion.4
  488.6 11.7 %cholesky.524 = f32[128,128]{1,0:T(8,128)S(1)} custom-call(f32[128,128]{1,0:T(8,128)S(1)} %cholesky.601), custom_call_target="Cholesky" | custom-call | tf_op jit(solution)/shard_map/jit(cholesky)/cholesky | solution.py:29
  501.1 9.8 %custom-call.69 = f32[1,128,128]{1,2,0:T(8,128)S(1)} custom-call(f32[1,128,128]{2,1,0:T(8,128)S(1)} %get-tuple-element.30), custom_call_target="InvertDiagBlocksLowerTriangular" | custom-call | tf_op jit(solution)/shard_map/jit(cholesky)/cholesky | solution.py:29
  511.9 3.1 convolution_subtract_fusion.5
  515.0 11.7 %cholesky.544 = f32[128,128]{1,0:T(8,128)S(1)} custom-call(f32[128,128]{1,0:T(8,128)S(1)} %cholesky.606), custom_call_target="Cholesky" | custom-call | tf_op jit(solution)/shard_map/jit(cholesky)/cholesky | solution.py:29
  527.5 9.8 %custom-call.70 = f32[1,128,128]{1,2,0:T(8,128)S(1)} custom-call(f32[1,128,128]{2,1,0:T(8,128)S(1)} %get-tuple-element.28), custom_call_target="InvertDiagBlocksLowerTriangular" | custom-call | tf_op jit(solution)/shard_map/jit(cholesky)/cholesky | solution.py:29
  538.2 2.1 convolution_subtract_fusion.6
  540.3 11.7 %cholesky.562 = f32[128,128]{1,0:T(8,128)S(1)} custom-call(f32[128,128]{1,0:T(8,128)S(1)} %convolution_subtract_fusion.6), custom_call_target="Cholesky" | custom-call | tf_op jit(solution)/shard_map/jit(cholesky)/cholesky | solution.py:29
  562.2 4.9 select_select_fusion
  567.1 24.5 %while.1 = (s32[]{:T(128)}, f32[1024,1024]{0,1:T(8,128)}, s32[8,2]{0,1:T(2,128)S(1)}, f32[8,128,128]{2,1,0:T(8,128)S(1)}, s32[]{:T(128)}) while((s32[]{:T(128)}, f32[1024,1024]{0,1:T(8,128)}, s32[8,2]{0,1:T(2,128)S(1)}, f32[8,128,128]{2,1,0:T(8,128)S(1)}, s32[]{:T(128)}) %tuple.49), condition=%wide.while_cond, body=%wide.while_body.sunk | while | flops 2 | bytes 393329 | solution.py:31
  567.8 2.3 dynamic-slice.8
  570.8 2.3 dynamic-slice.8
  573.9 2.3 dynamic-slice.8
  577.0 2.3 dynamic-slice.8
  580.0 2.3 dynamic-slice.8
  583.1 2.3 dynamic-slice.8
  586.2 2.3 dynamic-slice.8
  589.2 2.2 dynamic-slice.8
  591.6 78.8 %custom-call.71 = f32[8,128,128]{1,2,0:T(8,128)S(1)} custom-call(f32[8,128,128]{2,1,0:T(8,128)S(1)} %get-tuple-element.12), custom_call_target="InvertDiagBlocksLowerTriangular" | custom-call | tf_op jit(solution)/shard_map/triangular_solve | solution.py:31
  691.3 5.7 fusion.125
  697.6 63.9 %psum.15 = f32[]{:T(128)} all-reduce(f32[]{:T(128)} %multiply_reduce_fusion), channel_id=1, replica_groups=mesh['smp'=32,'col'=2,'slab'=2] {'smp','col','slab'}, use_global_device_ids=true, to_apply=%region_21.22 | all-reduce | flops 1 | bytes 8 | tf_op jit(solution)/shard_map/psum | solution.py:35
  (183 shorter events, 81.9 us)
Async XLA Ops:
  6.5 326.6 %all-reduce.4.cloned.1.call-start = ((), (), s32[]{:S(2)}) async-start(), calls=%async_computation.1 | async-start | bytes 8388608 | tf_op jit(solution)/shard_map/psum | solution.py:27
  141.9 3.2 copy-start
  155.2 23.5 %copy-start.3 = (u32[128]{0:T(128)S(1)}, u32[128]{0:T(128)}, u32[]{:S(2)}) copy-start(u32[128]{0:T(128)} %constant.323) | copy-start | bytes 1540
  155.2 24.7 %copy-start.2 = (f32[32]{0:T(128)S(1)}, f32[32]{0:T(128)}, u32[]{:S(2)}) copy-start(f32[32]{0:T(128)} %param.3) | copy-start | bytes 388
  351.4 2.0 copy-start.1
Sparse Core Ops, SparseCore 0:
  178.8 154.3 all-reduce.3
